TPU v7x, 256 devices: a whole 4x4x8 slice. The times are simulated.
256 devices in a mesh: seq: 64 (over y, z, core), head: 4 (over x).
Axes of the slice: x: 4, y: 4, z: 8, core: 2. Of those that a mesh axis runs over, the one named last changes fastest.
Arguments:
- queries: bfloat16 [32768, 2048], P('seq', 'head'), may hold values from -6 to 6
- keys: bfloat16 [32768, 2048], P('seq', 'head'), may hold values from -6 to 6
- values: bfloat16 [32768, 2048], P('seq', 'head'), may hold values from -6 to 6
- out_grad: bfloat16 [32768, 4096], P('seq', 'head'), may hold values from -16 to 16
- out_weight: bfloat16 [4096, 2048], P(None, 'head'), may hold values from -0.125 to 0.125
Outputs:
- query_grad: bfloat16 [32768, 2048], P('seq', 'head')
- key_grad: bfloat16 [32768, 2048], P('seq', 'head')
- value_grad: bfloat16 [32768, 2048], P('seq', 'head')
- weight_grad: float32 [4096, 2048], P('seq', 'head')
All inputs are finite; a program needn't handle non-finite values.
Results may differ from a plain program's by a relative error of at most 0.0058.
Values may be sent and summed in bfloat16 or wider, within the bound.
A program may use at most 128 MiB of HBM per device.

v0:
```python
import math
import jax
import jax.numpy as jnp
from jax import lax
from jax.sharding import PartitionSpec as P

HD = 128


def prefix(shard, axis, combine, identity):
    length, mine = (lax.axis_size(axis), lax.axis_index(axis))
    everything = lax.all_gather(shard, axis)
    start = jnp.broadcast_to(jnp.asarray(identity, shard.dtype), shard.shape)

    def turn(k, before):
        at = length - 1 - k
        reached = at > mine
        new = combine(before, everything[at])
        return jnp.where(reached, new, before)

    return lax.fori_loop(0, length, turn, start)


def add_states(earlier, later_part):
    return earlier + later_part


def per_device(queries, keys, values, out_grad, out_weight):
    rows = queries.shape[0]
    local_heads = queries.shape[1] // HD
    total = lax.axis_size("seq") * rows
    scale = 1.0 / math.sqrt(HD * total)
    full_grad = lax.all_gather(out_grad, "head", axis=1, tiled=True)
    attn_grad = jnp.dot(full_grad, out_weight, preferred_element_type=jnp.float32).astype(
        jnp.bfloat16
    )
    shape = (rows, local_heads, HD)
    query = queries.reshape(shape)
    key = keys.reshape(shape)
    value = values.reshape(shape)
    dout = attn_grad.reshape(shape)
    kv_term = scale * jnp.einsum("tha,thb->hab", key, value, preferred_element_type=jnp.float32)
    back_term = scale * jnp.einsum("tha,thb->hab", query, dout, preferred_element_type=jnp.float32)
    zeros = jnp.zeros_like(kv_term)
    position = lax.axis_index("seq")
    piece = lax.all_gather(kv_term[None], "seq", axis=0, tiled=True)
    index = jnp.arange(piece.shape[0], dtype=jnp.int32)
    keep = (index < position).astype(jnp.float32)
    prior_sum = jnp.sum(piece * keep[:, None, None, None], axis=0)
    later_sum = prefix(back_term, "seq", add_states, zeros)
    prior = prior_sum.astype(jnp.bfloat16)
    later = later_sum.astype(jnp.bfloat16)
    mask = jnp.tril(jnp.ones((rows, rows), jnp.float32))
    probs = (
        scale * jnp.einsum("tha,sha->hts", query, key, preferred_element_type=jnp.float32) * mask
    ).astype(jnp.bfloat16)
    grads = (
        scale * jnp.einsum("thb,shb->hts", dout, value, preferred_element_type=jnp.float32) * mask
    ).astype(jnp.bfloat16)
    outputs = (
        jnp.einsum("hts,shb->thb", probs, value, preferred_element_type=jnp.float32)
        + jnp.einsum("tha,hab->thb", query, prior, preferred_element_type=jnp.float32)
    ).astype(jnp.bfloat16)
    query_grad = (
        jnp.einsum("hts,sha->tha", grads, key, preferred_element_type=jnp.float32)
        + jnp.einsum("thb,hab->tha", dout, prior, preferred_element_type=jnp.float32)
    ).astype(jnp.bfloat16)
    key_grad = (
        jnp.einsum("hts,tha->sha", grads, query, preferred_element_type=jnp.float32)
        + jnp.einsum("shb,hab->sha", value, later, preferred_element_type=jnp.float32)
    ).astype(jnp.bfloat16)
    value_grad = (
        jnp.einsum("hts,thb->shb", probs, dout, preferred_element_type=jnp.float32)
        + jnp.einsum("sha,hab->shb", key, later, preferred_element_type=jnp.float32)
    ).astype(jnp.bfloat16)
    flat_out = outputs.reshape(rows, local_heads * HD)
    factor = 1.0 / math.sqrt(total)
    product = lax.dot_general(
        full_grad, flat_out, (((0,), (0,)), ((), ())), preferred_element_type=jnp.float32
    )
    weight_grad = lax.psum_scatter(product * factor, "seq", scatter_dimension=0, tiled=True)
    flat = (rows, local_heads * HD)
    return (query_grad.reshape(flat), key_grad.reshape(flat), value_grad.reshape(flat), weight_grad)


def solution(mesh):
    return jax.shard_map(
        per_device,
        mesh=mesh,
        in_specs=(
            P("seq", "head"),
            P("seq", "head"),
            P("seq", "head"),
            P("seq", "head"),
            P(None, "head"),
        ),
        out_specs=(P("seq", "head"), P("seq", "head"), P("seq", "head"), P("seq", "head")),
        check_vma=False,
    )
```

profile of v0, /device:TPU:2, one launch (start us, length us, event | category | flops | bytes accessed | tf_op | source)
XLA Modules:
  0.0 426.9 jit_solution(13473758385437747828)
XLA Ops:
  8.0 1.3 copy.57
  9.2 2.1 convolution_multiply_fusion.1
  11.4 51.5 %all-gather.6.cloned.1.call-done = bf16[512,4096]{1,0:T(8,128)(2,1)} async-done(((bf16[512,1024]{1,0:T(8,128)(2,1)}), bf16[512,4096]{1,0:T(8,128)(2,1)}) %all-gather.6.cloned.1.call-update) | async-done | bytes 4194320 | tf_op jit(solution)/shard_map/all_gather | solution.py:33
  62.9 5.8 %convolution_convert_fusion = bf16[512,512]{0,1:T(8,128)(2,1)S(1)} fusion(bf16[512,4096]{1,0:T(8,128)(2,1)} %all-gather.6.cloned.1.call-done, bf16[4096,512]{1,0:T(8,128)(2,1)} %param.11), kind=kOutput, calls=%fused_computation.15 | convolution fusion | flops 2147745792 | bytes 8912896 | tf_op jit(solution)/shard_map/dot_general | solution.py:34
  71.0 1.8 convolution_bitcast_fusion.1
  73.5 1.5 convolution_bitcast_fusion
  75.0 1.8 convolution_bitcast_fusion.2
  77.3 89.2 %all-gather.8.cloned.1.call-done = f32[256,128,128]{2,1,0:T(8,128)} async-done(((f32[4,128,128]{2,1,0:T(8,128)}), f32[256,128,128]{2,1,0:T(8,128)}) %all-gather.8.cloned.1.call-update) | async-done | bytes 16777232 | tf_op jit(solution)/shard_map/all_gather | solution.py:46
  166.5 7.7 %multiply_reduce_fusion = bf16[4,128,128]{2,1,0:T(8,128)(2,1)S(1)} fusion(f32[64,4,128,128]{3,2,1,0:T(8,128)} %bitcast.105, f32[64]{0:T(128)S(1)} %compare_convert_fusion), kind=kLoop, calls=%fused_computation.1 | loop fusion | flops 8323072 | bytes 16908544 | tf_op jit(solution)/shard_map/reduce_sum | solution.py:49
  174.3 1.1 fusion.3
  175.4 2.0 copy.47
  177.4 1.6 fusion.6
  179.0 8.0 %multiply_bitcast_fusion = f32[4096,512]{0,1:T(8,128)} fusion(bf16[512,512]{0,1:T(8,128)(2,1)S(1)} %bitcast.114, bf16[512,4096]{1,0:T(8,128)(2,1)} %all-gather.6.cloned.1.call-done), kind=kOutput, calls=%fused_computation.2 | convolution fusion | flops 2149580800 | bytes 13107200 | tf_op jit(solution)/shard_map/dot_general | solution.py:78
  187.0 9.0 %copy.55 = f32[4096,512]{1,0:T(8,128)} copy(f32[4096,512]{0,1:T(8,128)} %multiply_bitcast_fusion) | data formatting | bytes 16777216
  196.0 70.1 %all-gather.10.cloned.1.call-done = f32[256,128,128]{2,1,0:T(8,128)} async-done(((f32[4,128,128]{2,1,0:T(8,128)}), f32[256,128,128]{2,1,0:T(8,128)}) %all-gather.10.cloned.1.call-update) | async-done | bytes 16777232 | tf_op jit(solution)/shard_map/all_gather | solution.py:12
  266.1 68.7 %while.16 = (s32[]{:T(128)}, f32[4,128,128]{2,1,0:T(8,128)S(1)}, s32[]{:T(128)}, f32[64,4,128,128]{3,2,1,0:T(8,128)}, s32[]{:T(128)}, /*index=5*/s32[]{:T(128)}, s32[]{:T(128)}, s32[]{:T(128)}) while((s32[]{:T(128)}, f32[4,128,128]{2,1,0:T(8,128)S(1)}, s32[]{:T(128)}, f32[64,4,128,128]{3,2,1,0:T(8,128)}, s32[]{:T(128)}, ...), condition=%wide.region_2.3_spmd.clone, body=%wide.region_1.2_spmd.clone.sunk | while | flops 196616 | bytes 786595 | solution.py:21
  277.9 1.1 add_select_fusion.2
  288.6 1.1 add_select_fusion.2
  289.7 1.0 add_select_fusion.2
  290.8 1.1 add_select_fusion.2
  291.9 1.0 add_select_fusion.2
  293.0 1.1 add_select_fusion.2
  294.1 1.0 add_select_fusion.2
  296.2 1.0 add_select_fusion.2
  309.1 1.1 add_select_fusion.2
  310.2 1.0 add_select_fusion.2
  311.3 1.1 add_select_fusion.2
  313.4 1.1 add_select_fusion.2
  314.5 1.0 add_select_fusion.2
  315.6 1.1 add_select_fusion.2
  334.9 1.5 fusion.4
  338.8 81.6 %reduce-scatter.4.cloned.1.call-done = f32[64,512]{1,0:T(8,128)} async-done(((f32[4096,512]{1,0:T(8,128)}), f32[64,512]{1,0:T(8,128)}) %reduce-scatter.4.cloned.1.call-update) | async-done | bytes 131088
  (75 shorter events, 58.8 us)
Async XLA Ops:
  7.2 61.6 %copy-start = (bf16[512,512]{1,0:T(8,128)(2,1)S(1)}, bf16[512,512]{1,0:T(8,128)(2,1)}, u32[]{:S(2)}) copy-start(bf16[512,512]{1,0:T(8,128)(2,1)} %param.7) | copy-start | bytes 1572868
  7.2 55.7 %all-gather.6.cloned.1.call-start = ((), (), s32[]{:S(2)}) async-start(), calls=%async_computation.1 | async-start | bytes 5242880 | tf_op jit(solution)/shard_map/all_gather | solution.py:33
  7.9 158.6 %all-gather.8.cloned.1.call-start = ((), (), s32[]{:S(2)}) async-start(), calls=%async_computation.2 | async-start | bytes 17039360 | tf_op jit(solution)/shard_map/all_gather | solution.py:46
  11.3 58.9 %copy-start.1 = (bf16[512,512]{1,0:T(8,128)(2,1)S(1)}, bf16[512,512]{1,0:T(8,128)(2,1)}, u32[]{:S(2)}) copy-start(bf16[512,512]{1,0:T(8,128)(2,1)} %param.8) | copy-start | bytes 1572868
  11.4 254.8 %all-gather.10.cloned.1.call-start = ((), (), s32[]{:S(2)}) async-start(), calls=%async_computation.3 | async-start | bytes 17039360 | tf_op jit(solution)/shard_map/all_gather | solution.py:12
  69.9 350.4 %reduce-scatter.4.cloned.1.call-start = ((), (), s32[]{:S(2)}) async-start(), calls=%async_computation.4 | async-start | bytes 8519680
  166.5 7.8 %copy-start.2 = (f32[512,4,128]{0,2,1:T(8,128)S(1)}, f32[512,4,128]{0,2,1:T(8,128)}, u32[]{:S(2)}) copy-start(f32[512,4,128]{0,2,1:T(8,128)} %convolution_bitcast_fusion.2) | copy-start | bytes 3145732
Sparse Core Ops, SparseCore 0:
  9.8 53.0 all-gather.5
  66.2 100.2 all-gather.7
  169.9 96.2 all-gather.9
  270.8 149.5 reduce-scatter.3
where the time goes:
time: 429 us; the launch traced here: 427 us
  waiting for transfers between devices  293 us (68%)
  other arithmetic  74.8 us (17%)
  matrix products  27.7 us (6%)
  local copies, waits for them, and re-layouts  15.2 us (4%)
  between operations  13.9 us (3%)
    all_gather x1, waiting for transfers between devices, per_device(): piece = lax.all_gather(kv_term[None], 'seq', axis=0, tiled=True)  89.2 us
    unnamed x5, waiting for transfers between devices  82.3 us
    all_gather x1, waiting for transfers between devices, prefix(): everything = lax.all_gather(shard, axis)  70.1 us
    select_n x64, other arithmetic, turn(): return jnp.where(reached, new, before)  67 us
    all_gather x1, waiting for transfers between devices, per_device(): full_grad = lax.all_gather(out_grad, 'head', axis=1, tiled=True)  51.5 us
    unnamed x10, local copies, waits for them, and re-layouts  13.1 us
  transfers between devices with their start and end apart: 4, of which 4 were waited for; matrix products, arithmetic and copies ran while one was open for 28% of the time, Pallas kernels for 0%

commit v1 on v0

--- a/solution.py
+++ b/solution.py
@@ -1,3 +1,4 @@
+import functools
 import math
 import jax
 import jax.numpy as jnp
@@ -5,6 +6,38 @@
 from jax.sharding import PartitionSpec as P
 
 HD = 128
+
+
+def check_lanes_now(arr, dev_axis):
+    a_now = lax.axis_size(dev_axis)
+    placed = lax.axis_index(dev_axis)
+    reply, shaped, found_now = (a_now, placed, arr.shape[1])
+    frames = []
+    for h, p in enumerate(arr.shape):
+        frames.append(p * reply if h == 1 else p)
+    val = jnp.zeros(frames, arr.dtype)
+    answer = lax.dynamic_update_slice_in_dim(val, arr, shaped * found_now, axis=1)
+    tile_out = block_next = arr
+    for jj in range(1, reply // 2 + 1):
+        found = []
+        for h in range(reply):
+            found.append((h, (h + 1) % reply))
+        tile_out = lax.ppermute(tile_out, axis_name=dev_axis, perm=found)
+        answer = lax.dynamic_update_slice_in_dim(
+            answer, tile_out, (shaped - jj) % reply * found_now, axis=1
+        )
+        if 2 * jj < reply:
+            by_place = []
+            for h in range(reply):
+                by_place.append((h, (h - 1) % reply))
+            block_next = lax.ppermute(block_next, axis_name=dev_axis, perm=by_place)
+            answer = lax.dynamic_update_slice_in_dim(
+                answer, block_next, (shaped + jj) % reply * found_now, axis=1
+            )
+    return answer
+
+
+wait_lanes = functools.partial(check_lanes_now, dev_axis="head")
 
 
 def prefix(shard, axis, combine, identity):
@@ -30,7 +63,7 @@
     local_heads = queries.shape[1] // HD
     total = lax.axis_size("seq") * rows
     scale = 1.0 / math.sqrt(HD * total)
-    full_grad = lax.all_gather(out_grad, "head", axis=1, tiled=True)
+    full_grad = wait_lanes(out_grad)
     attn_grad = jnp.dot(full_grad, out_weight, preferred_element_type=jnp.float32).astype(
         jnp.bfloat16
     )

time: 429 us -> 376 us (0.88)
  waiting for transfers between devices: 293 us -> 245 us
  local copies, waits for them, and re-layouts: 15.2 us -> 9.87 us
    unnamed x5 -> x3, waiting for transfers between devices: 82.3 us -> 0.05 us
    reduce_scatter x0 -> x1, waiting for transfers between devices: none -> 81.6 us  [per_device(): lax.psum_scatter(product * factor, 'seq', scatter_dimension=0, tiled=True)]
    all_gather x1 -> x0, waiting for transfers between devices: 51.5 us -> none  [per_device(): full_grad = lax.all_gather(out_grad, 'head', axis=1, tiled=True)]
    all_gather x1, waiting for transfers between devices: 89.2 us -> 41.3 us  [per_device(): piece = lax.all_gather(kv_term[None], 'seq', axis=0, tiled=True)]
    ppermute x0 -> x3, waiting for transfers between devices: none -> 43 us  [the longest x2 43 us: check_lanes_now(): tile_out = lax.ppermute(tile_out, axis_name=dev_axis, perm=found)]
    all_gather x1, waiting for transfers between devices: 70.1 us -> 79.2 us  [prefix(): everything = lax.all_gather(shard, axis)]
    unnamed x10 -> x15, local copies, waits for them, and re-layouts: 13.1 us -> 4.09 us
  transfers between devices with their start and end apart: 4 -> 6, of which waited for: 4 -> 5; matrix products, arithmetic and copies ran while one was open for 28% -> 28% of each run, Pallas kernels for 0% -> 0%
where the time goes in v1:
time: 376 us; the launch traced here: 374 us
  waiting for transfers between devices  245 us (65%)
  other arithmetic  74.8 us (20%)
  matrix products  24.2 us (6%)
  between operations  14 us (4%)
  local copies, waits for them, and re-layouts  9.87 us (3%)
  starting transfers between devices  4.2 us (1%)
    reduce_scatter x1, waiting for transfers between devices, per_device(): lax.psum_scatter(product * factor, 'seq', scatter_dimension=0, tiled=True)  81.6 us
    all_gather x1, waiting for transfers between devices, prefix(): everything = lax.all_gather(shard, axis)  79.2 us
    select_n x64, other arithmetic, turn(): return jnp.where(reached, new, before)  67 us
    ppermute x2, waiting for transfers between devices, check_lanes_now(): tile_out = lax.ppermute(tile_out, axis_name=dev_axis, perm=found)  43 us
    all_gather x1, waiting for transfers between devices, per_device(): piece = lax.all_gather(kv_term[None], 'seq', axis=0, tiled=True)  41.3 us
    dot_general x1, matrix products, per_device(): lax.dot_general(full_grad, flat_out, (((0,), (0,)), ((), ())), preferred_...  7.96 us
    reduce_sum x1, other arithmetic, per_device(): prior_sum = jnp.sum(piece * keep[:, None, None, None], axis=0)  7.74 us
  transfers between devices with their start and end apart: 6, of which 5 were waited for; matrix products, arithmetic and copies ran while one was open for 28% of the time, Pallas kernels for 0%

profile of v1, /device:TPU:2, one launch (start us, length us, event | category | flops | bytes accessed | tf_op | source)
XLA Modules:
  0.0 374.1 jit_solution(11269373991708345745)
XLA Ops:
  7.2 1.4 copy.53
  8.6 2.1 convolution_multiply_fusion.2
  10.8 1.6 collective-permute-start
  13.2 22.8 %collective-permute-done = bf16[512,1024]{1,0:T(8,128)(2,1)S(1)} collective-permute-done((bf16[512,1024]{1,0:T(8,128)(2,1)}, bf16[512,1024]{1,0:T(8,128)(2,1)S(1)}, u32[]{:S(2)}, u32[]{:S(2)}) %collective-permute-start) | collective-permute-done | bytes 1048608 | tf_op jit(solution)/shard_map/ppermute | solution.py:25
  36.0 1.5 collective-permute-start.2
  38.2 1.5 constant_dynamic-update-slice_fusion.1
  39.8 20.2 %collective-permute-done.2 = bf16[512,1024]{1,0:T(8,128)(2,1)} collective-permute-done((bf16[512,1024]{1,0:T(8,128)(2,1)S(1)}, bf16[512,1024]{1,0:T(8,128)(2,1)}, u32[]{:S(2)}, u32[]{:S(2)}) %collective-permute-start.2) | collective-permute-done | bytes 1048608 | tf_op jit(solution)/shard_map/ppermute | solution.py:25
  60.0 1.3 constant_dynamic-update-slice_fusion
  61.4 2.4 convolution_convert_fusion
  66.0 1.7 convolution_bitcast_fusion.1
  67.8 1.4 fusion.28
  70.5 1.8 convolution_bitcast_fusion.2
  72.3 41.3 %all-gather.5.cloned.1.call-done = f32[256,128,128]{2,1,0:T(8,128)} async-done(((f32[4,128,128]{2,1,0:T(8,128)}), f32[256,128,128]{2,1,0:T(8,128)}) %all-gather.5.cloned.1.call-update) | async-done | bytes 16777232 | tf_op jit(solution)/shard_map/all_gather | solution.py:79
  113.6 7.7 %multiply_reduce_fusion = bf16[4,128,128]{2,1,0:T(8,128)(2,1)S(1)} fusion(f32[64,4,128,128]{3,2,1,0:T(8,128)} %bitcast.102, f32[64]{0:T(128)S(1)} %compare_convert_fusion), kind=kLoop, calls=%fused_computation.1 | loop fusion | flops 8323072 | bytes 16908544 | tf_op jit(solution)/shard_map/reduce_sum | solution.py:82
  121.3 1.1 fusion.3
  122.4 2.0 copy.46
  124.5 1.6 fusion.6
  126.0 8.0 %convolution_multiply_fusion = f32[4096,512]{1,0:T(8,128)} fusion(bf16[512,4096]{1,0:T(8,128)(2,1)} %copy-done.1, bf16[512,512]{0,1:T(8,128)(2,1)S(1)} %bitcast.111), kind=kOutput, calls=%fused_computation.2 | convolution fusion | flops 2149580800 | bytes 13107200 | tf_op jit(solution)/shard_map/dot_general | solution.py:111
  134.0 79.2 %all-gather.7.cloned.1.call-done = f32[256,128,128]{2,1,0:T(8,128)} async-done(((f32[4,128,128]{2,1,0:T(8,128)}), f32[256,128,128]{2,1,0:T(8,128)}) %all-gather.7.cloned.1.call-update) | async-done | bytes 16777232 | tf_op jit(solution)/shard_map/all_gather | solution.py:45
  213.2 68.9 %while.16 = (s32[]{:T(128)}, f32[4,128,128]{2,1,0:T(8,128)S(1)}, s32[]{:T(128)}, f32[64,4,128,128]{3,2,1,0:T(8,128)}, s32[]{:T(128)}, /*index=5*/s32[]{:T(128)}, s32[]{:T(128)}, s32[]{:T(128)}) while((s32[]{:T(128)}, f32[4,128,128]{2,1,0:T(8,128)S(1)}, s32[]{:T(128)}, f32[64,4,128,128]{3,2,1,0:T(8,128)}, s32[]{:T(128)}, ...), condition=%wide.region_2.3_spmd.clone, body=%wide.region_1.2_spmd.clone.sunk | while | flops 196616 | bytes 786587 | solution.py:54
  225.0 1.1 add_select_fusion.2
  227.1 1.0 add_select_fusion.2
  228.2 1.1 add_select_fusion.2
  230.4 1.1 add_select_fusion.2
  244.4 1.1 add_select_fusion.2
  246.5 1.1 add_select_fusion.2
  248.7 1.1 add_select_fusion.2
  264.9 1.1 add_select_fusion.2
  267.0 1.1 add_select_fusion.2
  269.2 1.1 add_select_fusion.2
  282.1 1.6 fusion.5
  285.9 81.6 %reduce-scatter.2.cloned.1.call-done = f32[64,512]{1,0:T(8,128)} async-done(((f32[4096,512]{1,0:T(8,128)}), f32[64,512]{1,0:T(8,128)}) %reduce-scatter.2.cloned.1.call-update) | async-done | bytes 131088 | tf_op jit(solution)/shard_map/reduce_scatter | solution.py:114
  (88 shorter events, 63.9 us)
Async XLA Ops:
  7.2 56.6 %copy-start = (bf16[512,512]{1,0:T(8,128)(2,1)S(1)}, bf16[512,512]{1,0:T(8,128)(2,1)}, u32[]{:S(2)}) copy-start(bf16[512,512]{1,0:T(8,128)(2,1)} %param.7) | copy-start | bytes 1572868
  7.2 30.8 %copy-start.4 = (bf16[512,1024]{1,0:T(8,128)(2,1)S(1)}, bf16[512,1024]{1,0:T(8,128)(2,1)}, u32[]{:S(2)}) copy-start(bf16[512,1024]{1,0:T(8,128)(2,1)} %param.10) | copy-start | bytes 3145732
  7.2 106.4 %all-gather.5.cloned.1.call-start = ((), (), s32[]{:S(2)}) async-start(), calls=%async_computation.2 | async-start | bytes 17039360 | tf_op jit(solution)/shard_map/all_gather | solution.py:79
  10.7 202.5 %all-gather.7.cloned.1.call-start = ((), (), s32[]{:S(2)}) async-start(), calls=%async_computation.3 | async-start | bytes 17039360 | tf_op jit(solution)/shard_map/all_gather | solution.py:45
  10.8 25.2 %collective-permute-start = (bf16[512,1024]{1,0:T(8,128)(2,1)}, bf16[512,1024]{1,0:T(8,128)(2,1)S(1)}, u32[]{:S(2)}, u32[]{:S(2)}) collective-permute-start(bf16[512,1024]{1,0:T(8,128)(2,1)} %param.10), channel_id=1, source_target_pairs={{0,1},{1,2},{2,3},{3,0},{4,5},{5,6},{6,7},{7,4},{8,9},{9,10},{10,1... | collective-permute-start | bytes 3145736 | tf_op jit(solution)/shard_map/ppermute | solution.py:25
  12.3 25.9 %collective-permute-start.1 = (bf16[512,1024]{1,0:T(8,128)(2,1)}, bf16[512,1024]{1,0:T(8,128)(2,1)}, u32[]{:S(2)}, u32[]{:S(2)}) collective-permute-start(bf16[512,1024]{1,0:T(8,128)(2,1)} %param.10), channel_id=1, source_target_pairs={{0,3},{1,0},{2,1},{3,2},{4,7},{5,4},{6,5},{7,6},{8,11},{9,8},{10,9... | collective-permute-start | bytes 3145736 | tf_op jit(solution)/shard_map/ppermute | solution.py:33
  36.0 24.0 %collective-permute-start.2 = (bf16[512,1024]{1,0:T(8,128)(2,1)S(1)}, bf16[512,1024]{1,0:T(8,128)(2,1)}, u32[]{:S(2)}, u32[]{:S(2)}) collective-permute-start(bf16[512,1024]{1,0:T(8,128)(2,1)S(1)} %collective-permute-done), channel_id=1, source_target_pairs={{0,1},{1,2},{2,3},{3,0},{4,5},{5,6},{6,7},{7,4},{8,9},{9,10},{10,1... | collective-permute-start | bytes 3145736 | tf_op jit(solution)/shard_map/ppermute | solution.py:25
  38.0 23.4 %copy-start.5 = (bf16[4096,512]{1,0:T(8,128)(2,1)S(1)}, bf16[4096,512]{1,0:T(8,128)(2,1)}, u32[]{:S(2)}) copy-start(bf16[4096,512]{1,0:T(8,128)(2,1)} %param.11) | copy-start | bytes 12582916
  61.3 2.4 copy-start.1
  61.4 4.0 %copy-start.2 = (bf16[512,512]{1,0:T(8,128)(2,1)S(1)}, bf16[512,512]{1,0:T(8,128)(2,1)}, u32[]{:S(2)}) copy-start(bf16[512,512]{1,0:T(8,128)(2,1)} %param.8) | copy-start | bytes 1572868
  64.9 302.6 %reduce-scatter.2.cloned.1.call-start = ((), (), s32[]{:S(2)}) async-start(), calls=%async_computation.1 | async-start | bytes 8519680 | tf_op jit(solution)/shard_map/reduce_scatter | solution.py:114
  113.6 7.8 %copy-start.3 = (f32[512,4,128]{0,2,1:T(8,128)S(1)}, f32[512,4,128]{0,2,1:T(8,128)}, u32[]{:S(2)}) copy-start(f32[512,4,128]{0,2,1:T(8,128)} %convolution_bitcast_fusion.2) | copy-start | bytes 3145732
Sparse Core Ops, SparseCore 0:
  11.3 102.1 all-gather.4
  116.9 96.2 all-gather.6
  218.0 149.5 reduce-scatter.1
